TPU v7x, 32 devices: a whole 2x2x4 slice. The times are simulated.
32 devices in a mesh: dp: 16 (over z, y, core), tensor: 2 (over x).
Axes of the slice: x: 2, y: 2, z: 4, core: 2. Of those that a mesh axis runs over, the one named last changes fastest.
Arguments:
- tokens: bfloat16 [4096, 6144], P('dp', 'tensor'), may hold values from -6 to 6
- grad_out: bfloat16 [4096, 6144], P('dp', 'tensor'), may hold values from -6 to 6
- input_norm_gain: float32 [6144], replicated, may hold values from 0.1 to 1.9
- q_gain: float32 [128], replicated, may hold values from 0.1 to 1.9
- k_gain: float32 [128], replicated, may hold values from 0.1 to 1.9
- w_qkv: bfloat16 [3, 6144, 3072], P(None, 'dp', 'tensor'), may hold values from -0.078125 to 0.078125
- w_out: bfloat16 [3072, 6144], P('tensor', 'dp'), may hold values from -0.109375 to 0.109375
- pattern: int32 [24, 4, 2], P('tensor'), may hold values from 0 to 3, all different within a row
Outputs:
- tokens_grad: bfloat16 [4096, 6144], P('dp', 'tensor')
All inputs are finite; a program needn't handle non-finite values.
Results may differ from a plain program's by a relative error of at most 0.015.
Values may be sent and summed in bfloat16 or wider, within the bound.
A program may use at most 192 MiB of HBM per device.

v0:
```python
import math
import jax
import jax.numpy as jnp
from jax import lax
from jax.sharding import PartitionSpec as P

HD = 128
SEQ = 256
BLK = 64


def norm_rows(values, gain):
    centre = jnp.mean(values, axis=-1, keepdims=True)
    centered_input = values - centre
    inverse_deviation = lax.rsqrt(
        jnp.mean(centered_input * centered_input, axis=-1, keepdims=True) + 1e-06
    )
    return centered_input * inverse_deviation * gain


def block_mask(pattern, seq_len, block):
    count = seq_len // block
    hits = pattern[:, :, :, None] == jnp.arange(count, dtype=jnp.int32)[None, None, None, :]
    allowed = jnp.any(hits, axis=2).astype(jnp.float32)
    heads = allowed.shape[0]
    spread = jnp.broadcast_to(allowed[:, :, None, :, None], (heads, count, block, count, block))
    return spread.reshape(heads, seq_len, seq_len)


def attention_grads(stacked, upstream, q_gain, k_gain, allowed):

    def attend(query, key, value):
        q_normed = norm_rows(query, q_gain)
        k_normed = norm_rows(key, k_gain)
        scores = jnp.einsum(
            "aqhd,akhd->ahqk", q_normed, k_normed, precision=lax.Precision.HIGHEST
        ) / math.sqrt(query.shape[-1])
        weights = jnp.exp(scores) * allowed[None]
        probs = weights / jnp.sum(weights, axis=-1, keepdims=True)
        return jnp.einsum("ahqk,akhd->aqhd", probs, value, precision=lax.Precision.HIGHEST)

    widened = stacked.astype(jnp.float32)
    _, pull = jax.vjp(attend, widened[0], widened[1], widened[2])
    grads = pull(upstream.astype(jnp.float32))
    return jnp.stack(grads).astype(jnp.bfloat16)


def body(tokens, grad_out, input_norm_gain, q_gain, k_gain, w_qkv, w_out, pattern):
    width = tokens.shape[1]
    row_count = tokens.shape[0]
    rows_full, grads_full = (
        lax.all_gather(tokens, "tensor", axis=1, tiled=True),
        lax.all_gather(grad_out, "tensor", axis=1, tiled=True),
    )
    values = rows_full.astype(jnp.float32)
    centre = jnp.mean(values, axis=-1, keepdims=True)
    centered_input = values - centre
    inverse_deviation = lax.rsqrt(
        jnp.mean(centered_input * centered_input, axis=-1, keepdims=True) + 1e-06
    )
    standardized_input = centered_input * inverse_deviation
    normalized_input = (standardized_input * input_norm_gain).astype(jnp.bfloat16)
    whole = lax.all_gather(w_qkv, "dp", axis=1, tiled=True)
    qkv = jnp.einsum(
        "rd,idh->irh", normalized_input, whole, preferred_element_type=jnp.float32
    ).astype(jnp.bfloat16)
    local_width = whole.shape[2]
    upstream = lax.dot_general(
        grads_full,
        lax.all_gather(w_out, "dp", axis=1, tiled=True),
        (((1,), (1,)), ((), ())),
        preferred_element_type=jnp.float32,
    ).astype(jnp.bfloat16)
    local_heads = local_width // HD
    images = row_count // SEQ
    allowed = block_mask(pattern, SEQ, BLK)
    d_qkv = attention_grads(
        qkv.reshape(3, images, SEQ, local_heads, HD),
        upstream.reshape(images, SEQ, local_heads, HD),
        q_gain,
        k_gain,
        allowed,
    )
    d_qkv = d_qkv.reshape(3, row_count, local_width)
    partial_grad = jnp.einsum("irh,idh->rd", d_qkv, whole, preferred_element_type=jnp.float32)
    offset = lax.axis_index("tensor") * width
    d_normed = lax.psum(partial_grad.astype(jnp.bfloat16), "tensor").astype(jnp.float32)
    normalized_gradient = d_normed * input_norm_gain
    leading_term = jnp.mean(normalized_gradient, axis=-1, keepdims=True)
    trailing_term = jnp.mean(normalized_gradient * standardized_input, axis=-1, keepdims=True)
    complete_gradient = inverse_deviation * (
        normalized_gradient - leading_term - standardized_input * trailing_term
    )
    result = lax.dynamic_slice_in_dim(complete_gradient, offset, width, 1)
    return result.astype(jnp.bfloat16)


def solution(mesh):
    return jax.shard_map(
        body,
        mesh=mesh,
        in_specs=(
            P("dp", "tensor"),
            P("dp", "tensor"),
            P(),
            P(),
            P(),
            P(None, "dp", "tensor"),
            P("tensor", "dp"),
            P("tensor", None, None),
        ),
        out_specs=P("dp", "tensor"),
        check_vma=False,
    )
```

profile of v0, /device:TPU:0, one launch (start us, length us, event | category | flops | bytes accessed | tf_op | source)
XLA Modules:
  0.0 674.1 jit_solution(7555071908021062251)
XLA Ops:
  9.5 3.6 broadcast_in_dim.14
  13.2 7.0 %broadcast_in_dim_reshape.3 = f32[12,256,256]{1,2,0:T(8,128)} reshape(f32[12,4,64,4,64]{2,1,4,3,0:T(4,128)} %broadcast_in_dim.14) | data formatting | bytes 6291456 | tf_op jit(solution)/shard_map/jvp()/broadcast_in_dim;reshape | solution.py:38
  20.2 36.4 %all-gather.5.cloned.1.call-done = bf16[256,6144]{1,0:T(8,128)(2,1)} async-done(((bf16[256,3072]{1,0:T(8,128)(2,1)}), bf16[256,6144]{1,0:T(8,128)(2,1)}) %all-gather.5.cloned.1.call-update) | async-done | bytes 3145744 | tf_op jit(solution)/shard_map/all_gather | solution.py:52
  56.6 2.5 convert_reduce_fusion
  60.4 42.7 %all-gather.7.cloned.1.call-done = bf16[256,6144]{1,0:T(8,128)(2,1)} async-done(((bf16[256,3072]{1,0:T(8,128)(2,1)}), bf16[256,6144]{1,0:T(8,128)(2,1)}) %all-gather.7.cloned.1.call-update) | async-done | bytes 3145744 | tf_op jit(solution)/shard_map/all_gather | solution.py:53
  103.1 100.4 %all-gather.9.cloned.1.call-done = bf16[1536,6144]{1,0:T(8,128)(2,1)} async-done(((bf16[1536,384]{1,0:T(8,128)(2,1)}), bf16[1536,6144]{1,0:T(8,128)(2,1)}) %all-gather.9.cloned.1.call-update) | async-done | bytes 18874384 | tf_op jit(solution)/shard_map/all_gather | solution.py:70
  203.5 10.6 %convolution_convert_fusion.1 = bf16[256,1536]{1,0:T(8,128)(2,1)} fusion(bf16[256,6144]{1,0:T(8,128)(2,1)} %all-gather.7.cloned.1.call-done, bf16[1536,6144]{1,0:T(8,128)(2,1)} %all-gather.9.cloned.1.call-done), kind=kOutput, calls=%fused_computation.25 | convolution fusion | flops 4832231424 | bytes 22806528 | tf_op jit(solution)/shard_map/dot_general | solution.py:68
  214.1 2.4 copy.40
  216.5 265.2 %all-gather.11.cloned.1.call-done = bf16[3,6144,1536]{2,1,0:T(8,128)(2,1)} async-done(((bf16[3,384,1536]{2,1,0:T(8,128)(2,1)}), bf16[3,6144,1536]{2,1,0:T(8,128)(2,1)}) %all-gather.11.cloned.1.call-update) | async-done | bytes 56623120 | tf_op jit(solution)/shard_map/all_gather | solution.py:63
  481.7 24.1 %fusion.12 = bf16[3,256,1536]{2,1,0:T(8,128)(2,1)} fusion(bf16[3,6144,1536]{2,1,0:T(8,128)(2,1)} %all-gather.11.cloned.1.call-done, f32[6144]{0:T(1024)S(1)} %copy-done.9, bf16[256,6144]{1,0:T(8,128)(2,1)S(1)} %copy-done.3, f32[256]{0:T(256)S(1)} %add_rsqrt_fusion, f32[256]{0:T(256)S(1)} %broadcast_multiply_fusion.4), kind=kOutput, calls=%fused_computation.23 | convolution fusion | flops 14504558592 | bytes 62154752 | tf_op jit(solution)/shard_map/rd,idh->irh/dot_general | solution.py:64
  505.8 2.9 fusion.50
  508.7 2.1 slice.15
  515.3 5.4 fusion.48
  520.7 2.3 copy.41
  523.0 6.4 fusion.25
  531.4 5.0 fusion.22
  536.5 3.5 fusion.23
  540.0 2.3 copy.55
  542.3 1.9 fusion.42
  545.6 2.4 copy.54
  551.2 24.2 %fusion = bf16[256,6144]{1,0:T(8,128)(2,1)} fusion(bf16[3,6144,1536]{2,1,0:T(8,128)(2,1)} %all-gather.11.cloned.1.call-done, bf16[1,256,1536]{2,1,0:T(8,128)(2,1)} %copy.55, bf16[1,256,1536]{2,1,0:T(8,128)(2,1)} %copy.54, bf16[1,256,1536]{2,1,0:T(8,128)(2,1)S(1)} %copy.53), kind=kOutput, calls=%fused_computation.3 | convolution fusion | flops 14499446784 | bytes 62128128 | tf_op jit(solution)/shard_map/irh,idh->rd/dot_general | solution.py:85
  575.4 85.8 %all-reduce.2.cloned.1.call-done = bf16[256,6144]{1,0:T(8,128)(2,1)} async-done(((bf16[256,6144]{1,0:T(8,128)(2,1)}), bf16[256,6144]{1,0:T(8,128)(2,1)}) %all-reduce.2.cloned.1.call-update) | async-done | bytes 3145744 | tf_op jit(solution)/shard_map/psum | solution.py:87
  661.3 4.1 fusion.16
  665.4 2.2 fusion.8
  (65 shorter events, 15.1 us)
Async XLA Ops:
  6.5 50.0 %all-gather.5.cloned.1.call-start = ((), (), s32[]{:S(2)}) async-start(), calls=%async_computation | async-start | bytes 4718592 | tf_op jit(solution)/shard_map/all_gather | solution.py:52
  7.3 95.8 %all-gather.7.cloned.1.call-start = ((), (), s32[]{:S(2)}) async-start(), calls=%async_computation.1 | async-start | bytes 4718592 | tf_op jit(solution)/shard_map/all_gather | solution.py:53
  8.0 1.4 copy-start.12
  8.0 195.5 %all-gather.9.cloned.1.call-start = ((), (), s32[]{:S(2)}) async-start(), calls=%async_computation.2 | async-start | bytes 20054016 | tf_op jit(solution)/shard_map/all_gather | solution.py:70
  8.8 472.9 %all-gather.11.cloned.1.call-start = ((), (), s32[]{:S(2)}) async-start(), calls=%async_computation.3 | async-start | bytes 60162048 | tf_op jit(solution)/shard_map/all_gather | solution.py:63
  9.3 651.9 %all-reduce.2.cloned.1.call-start = ((), (), s32[]{:S(2)}) async-start(), calls=%async_computation.4 | async-start | bytes 6291456 | tf_op jit(solution)/shard_map/psum | solution.py:87
  56.6 2.8 copy-start.3
  60.4 421.3 %copy-start.9 = (f32[6144]{0:T(1024)S(1)}, f32[6144]{0:T(1024)}, u32[]{:S(2)}) copy-start(f32[6144]{0:T(1024)} %param.10) | copy-start | bytes 73732
  513.3 0.7 copy-start.10
  513.3 0.7 copy-start.11
  513.4 1.9 copy-start
  523.0 6.5 copy-start.1
  523.0 6.5 copy-start.2
  523.0 6.5 copy-start.7
  523.0 6.5 copy-start.8
  542.3 2.0 copy-start.6
  545.6 2.4 copy-start.5
  575.4 85.9 %copy-start.4 = (bf16[256,6144]{1,0:T(8,128)(2,1)S(1)}, bf16[256,6144]{1,0:T(8,128)(2,1)}, u32[]{:S(2)}) copy-start(bf16[256,6144]{1,0:T(8,128)(2,1)} %all-gather.5.cloned.1.call-done) | copy-start | bytes 9437188
Sparse Core Ops, SparseCore 0:
  8.9 47.6 all-gather.4
  58.1 44.9 all-gather.6
  104.6 98.8 all-gather.8
  204.9 276.7 all-gather.10
  575.5 85.6 all-reduce.1
where the time goes:
time: 675 us; the launch traced here: 674 us
  waiting for transfers between devices  533 us (79%)
  matrix products  80.3 us (12%)
  local copies, waits for them, and re-layouts  30.7 us (5%)
  other arithmetic  16.4 us (2%)
  between operations  13.4 us (2%)
    all_gather x1, waiting for transfers between devices, body(): whole = lax.all_gather(w_qkv, 'dp', axis=1, tiled=True)  265 us
    all_gather x1, waiting for transfers between devices, body(): lax.all_gather(w_out, 'dp', axis=1, tiled=True)  100 us
    psum x1, waiting for transfers between devices, body(): lax.psum(partial_grad.astype(jnp.bfloat16), 'tensor').astype(jnp.float32)  85.8 us
    all_gather x1, waiting for transfers between devices, body(): lax.all_gather(grad_out, 'tensor', axis=1, tiled=True)  42.7 us
    all_gather x1, waiting for transfers between devices, body(): lax.all_gather(tokens, 'tensor', axis=1, tiled=True)  36.4 us
    dot_general x1, matrix products, body(): jnp.einsum('irh,idh->rd', d_qkv, whole, preferred_element_type=jnp.float32)  24.2 us
    dot_general x1, matrix products, body(): jnp.einsum('rd,idh->irh', normalized_input, whole, preferred_element_type...  24.1 us
    dot_general x3, matrix products, attend(): jnp.einsum('aqhd,akhd->ahqk', q_normed, k_normed, precision=lax.Precision...  14 us
  transfers between devices with their start and end apart: 5, of which 5 were waited for; matrix products, arithmetic and copies ran while one was open for 4% of the time, Pallas kernels for 0%

commit v1 on v0

--- a/solution.py
+++ b/solution.py
@@ -7,6 +7,13 @@
 HD = 128
 SEQ = 256
 BLK = 64
+
+
+def all_by_exchange(x, axis, dim):
+    size = lax.axis_size(axis)
+    shards = jnp.stack([x for _ in range(size)])
+    shards = lax.all_to_all(shards, axis, split_axis=0, concat_axis=0)
+    return jnp.concatenate(shards, axis=dim)
 
 
 def norm_rows(values, gain):
@@ -50,7 +57,7 @@
     row_count = tokens.shape[0]
     rows_full, grads_full = (
         lax.all_gather(tokens, "tensor", axis=1, tiled=True),
-        lax.all_gather(grad_out, "tensor", axis=1, tiled=True),
+        all_by_exchange(grad_out, "tensor", 1),
     )
     values = rows_full.astype(jnp.float32)
     centre = jnp.mean(values, axis=-1, keepdims=True)

time: 675 us -> 661 us (0.979)
  waiting for transfers between devices: 533 us -> 511 us
    all_gather x1 -> x0, waiting for transfers between devices: 42.7 us -> none  [body(): lax.all_gather(grad_out, 'tensor', axis=1, tiled=True)]
    all_gather x1, waiting for transfers between devices: 36.4 us -> 60.5 us  [body(): lax.all_gather(tokens, 'tensor', axis=1, tiled=True)]
  transfers between devices with their start and end apart: 5 -> 5, of which waited for: 5 -> 4; matrix products, arithmetic and copies ran while one was open for 4% -> 5% of each run, Pallas kernels for 0% -> 0%
where the time goes in v1:
time: 661 us; the launch traced here: 660 us
  waiting for transfers between devices  511 us (77%)
  matrix products  80.4 us (12%)
  local copies, waits for them, and re-layouts  31.5 us (5%)
  other arithmetic  18.4 us (3%)
  between operations  13.4 us (2%)
    all_gather x1, waiting for transfers between devices, body(): whole = lax.all_gather(w_qkv, 'dp', axis=1, tiled=True)  265 us
    all_gather x1, waiting for transfers between devices, body(): lax.all_gather(w_out, 'dp', axis=1, tiled=True)  97.2 us
    psum x1, waiting for transfers between devices, body(): lax.psum(partial_grad.astype(jnp.bfloat16), 'tensor').astype(jnp.float32)  85.9 us
    all_gather x1, waiting for transfers between devices, body(): lax.all_gather(tokens, 'tensor', axis=1, tiled=True)  60.5 us
    dot_general x1, matrix products, body(): jnp.einsum('irh,idh->rd', d_qkv, whole, preferred_element_type=jnp.float32)  24.2 us
    dot_general x1, matrix products, body(): jnp.einsum('rd,idh->irh', normalized_input, whole, preferred_element_type...  24.1 us
    dot_general x3, matrix products, attend(): jnp.einsum('aqhd,akhd->ahqk', q_normed, k_normed, precision=lax.Precision...  14 us
  transfers between devices with their start and end apart: 5, of which 4 were waited for; matrix products, arithmetic and copies ran while one was open for 5% of the time, Pallas kernels for 0%

profile of v1, /device:TPU:0, one launch (start us, length us, event | category | flops | bytes accessed | tf_op | source)
XLA Modules:
  0.0 660.0 jit_solution(11699399383068684348)
XLA Ops:
  9.5 2.0 pad_maximum_fusion
  11.4 5.3 all-to-all-start
  17.0 3.7 broadcast_in_dim.14
  20.7 7.0 %broadcast_in_dim_reshape.3 = f32[12,256,256]{1,2,0:T(8,128)} reshape(f32[12,4,64,4,64]{2,1,4,3,0:T(4,128)} %broadcast_in_dim.14) | data formatting | bytes 6291456 | tf_op jit(solution)/shard_map/jvp()/broadcast_in_dim;reshape | solution.py:45
  27.7 60.5 %all-gather.4.cloned.1.call-done = bf16[256,6144]{1,0:T(8,128)(2,1)} async-done(((bf16[256,3072]{1,0:T(8,128)(2,1)}), bf16[256,6144]{1,0:T(8,128)(2,1)}) %all-gather.4.cloned.1.call-update) | async-done | bytes 3145744 | tf_op jit(solution)/shard_map/all_gather | solution.py:59
  88.2 2.5 convert_reduce_fusion
  92.1 97.2 %all-gather.6.cloned.1.call-done = bf16[1536,6144]{1,0:T(8,128)(2,1)} async-done(((bf16[1536,384]{1,0:T(8,128)(2,1)}), bf16[1536,6144]{1,0:T(8,128)(2,1)}) %all-gather.6.cloned.1.call-update) | async-done | bytes 18874384 | tf_op jit(solution)/shard_map/all_gather | solution.py:77
  189.2 10.7 %convolution_convert_fusion.1 = bf16[256,1536]{1,0:T(8,128)(2,1)} fusion(bf16[256,6144]{0,1:T(8,128)(2,1)} %bitcast.2, bf16[1536,6144]{1,0:T(8,128)(2,1)} %all-gather.6.cloned.1.call-done), kind=kOutput, calls=%fused_computation.26 | convolution fusion | flops 4832231424 | bytes 22806528 | tf_op jit(solution)/shard_map/dot_general | solution.py:75
  199.9 2.4 copy.42
  202.3 265.2 %all-gather.8.cloned.1.call-done = bf16[3,6144,1536]{2,1,0:T(8,128)(2,1)} async-done(((bf16[3,384,1536]{2,1,0:T(8,128)(2,1)}), bf16[3,6144,1536]{2,1,0:T(8,128)(2,1)}) %all-gather.8.cloned.1.call-update) | async-done | bytes 56623120 | tf_op jit(solution)/shard_map/all_gather | solution.py:70
  467.5 24.1 %fusion.12 = bf16[3,256,1536]{2,1,0:T(8,128)(2,1)} fusion(bf16[3,6144,1536]{2,1,0:T(8,128)(2,1)} %all-gather.8.cloned.1.call-done, f32[6144]{0:T(1024)S(1)} %copy-done.10, bf16[256,6144]{1,0:T(8,128)(2,1)S(1)} %copy-done.3, f32[256]{0:T(256)S(1)} %add_rsqrt_fusion, f32[256]{0:T(256)S(1)} %broadcast_multiply_fusion.4), kind=kOutput, calls=%fused_computation.24 | convolution fusion | flops 14504558592 | bytes 62154752 | tf_op jit(solution)/shard_map/rd,idh->irh/dot_general | solution.py:71
  491.6 2.9 fusion.50
  494.5 2.1 slice.15
  501.1 5.4 fusion.48
  506.6 2.3 copy.43
  508.9 6.4 fusion.25
  517.3 5.0 fusion.22
  522.3 3.5 fusion.23
  525.8 2.3 copy.57
  531.5 2.4 copy.56
  537.0 24.2 %fusion = bf16[256,6144]{1,0:T(8,128)(2,1)} fusion(bf16[3,6144,1536]{2,1,0:T(8,128)(2,1)} %all-gather.8.cloned.1.call-done, bf16[1,256,1536]{2,1,0:T(8,128)(2,1)} %copy.57, bf16[1,256,1536]{2,1,0:T(8,128)(2,1)} %copy.56, bf16[1,256,1536]{2,1,0:T(8,128)(2,1)S(1)} %copy.55), kind=kOutput, calls=%fused_computation.3 | convolution fusion | flops 14499446784 | bytes 62128128 | tf_op jit(solution)/shard_map/irh,idh->rd/dot_general | solution.py:92
  561.3 85.9 %all-reduce.2.cloned.1.call-done = bf16[256,6144]{1,0:T(8,128)(2,1)} async-done(((bf16[256,6144]{1,0:T(8,128)(2,1)}), bf16[256,6144]{1,0:T(8,128)(2,1)}) %all-reduce.2.cloned.1.call-update) | async-done | bytes 3145744 | tf_op jit(solution)/shard_map/psum | solution.py:94
  647.2 4.1 fusion.16
  651.3 2.2 fusion.8
  (68 shorter events, 17.2 us)
Async XLA Ops:
  6.5 81.7 %all-gather.4.cloned.1.call-start = ((), (), s32[]{:S(2)}) async-start(), calls=%async_computation.1 | async-start | bytes 4718592 | tf_op jit(solution)/shard_map/all_gather | solution.py:59
  7.3 1.5 copy-start.9
  7.3 182.0 %all-gather.6.cloned.1.call-start = ((), (), s32[]{:S(2)}) async-start(), calls=%async_computation.2 | async-start | bytes 20054016 | tf_op jit(solution)/shard_map/all_gather | solution.py:77
  8.0 459.5 %all-gather.8.cloned.1.call-start = ((), (), s32[]{:S(2)}) async-start(), calls=%async_computation.3 | async-start | bytes 60162048 | tf_op jit(solution)/shard_map/all_gather | solution.py:70
  11.4 5.4 copy-start.13
  11.4 80.6 %all-to-all-start = ((bf16[2,256,3072]{1,2,0:T(8,128)(2,1)}), bf16[2,256,3072]{1,2,0:T(8,128)(2,1)}, u32[]{:S(2)}, u32[]{:S(2)}) async-start(bf16[2,256,3072]{1,2,0:T(8,128)(2,1)} %pad_maximum_fusion), calls=%async_computation | async-start | bytes 6291456 | tf_op jit(solution)/shard_map/all_to_all | solution.py:15
  16.8 630.4 %all-reduce.2.cloned.1.call-start = ((), (), s32[]{:S(2)}) async-start(), calls=%async_computation.4 | async-start | bytes 6291456 | tf_op jit(solution)/shard_map/psum | solution.py:94
  88.2 2.8 copy-start.3
  189.2 278.3 %copy-start.10 = (f32[6144]{0:T(1024)S(1)}, f32[6144]{0:T(1024)}, u32[]{:S(2)}) copy-start(f32[6144]{0:T(1024)} %param.10) | copy-start | bytes 73732
  499.1 0.7 copy-start.11
  499.1 0.7 copy-start.12
  499.2 1.9 copy-start
  508.8 6.5 copy-start.1
  508.9 6.5 copy-start.2
  508.9 6.5 copy-start.7
  508.9 6.5 copy-start.8
  528.1 2.0 copy-start.6
  531.5 2.4 copy-start.5
  561.2 85.9 %copy-start.4 = (bf16[256,6144]{1,0:T(8,128)(2,1)S(1)}, bf16[256,6144]{1,0:T(8,128)(2,1)}, u32[]{:S(2)}) copy-start(bf16[256,6144]{1,0:T(8,128)(2,1)} %all-gather.4.cloned.1.call-done) | copy-start | bytes 9437188
Sparse Core Ops, SparseCore 0:
  8.9 79.2 all-gather.3
  89.8 99.3 all-gather.5
  190.8 276.6 all-gather.7
  561.4 85.7 all-reduce.1
